TPU v7x, 32 devices: a whole 2x2x4 slice. The times are simulated.
32 devices in a mesh: occ: 16 (over z, y, core), vir: 2 (over x).
Axes of the slice: x: 2, y: 2, z: 4, core: 2. Of those that a mesh axis runs over, the one named last changes fastest.
Arguments:
- lambda_triples: bfloat16 [256, 320, 320], P('occ', 'vir'), may hold values from -6 to 6
- amplitude_triples: bfloat16 [256, 320, 320], P('occ', 'vir'), may hold values from -6 to 6
- spin_extent: int32 [256], P('occ'), may hold values from 80 to 320
- ladder_weight: bfloat16 [320, 320], P(None, 'vir'), may hold values from -0.3125 to 0.3125
- cycle_weight: bfloat16 [320, 40], replicated, may hold values from -0.3125 to 0.3125
- lambda_doubles: bfloat16 [40, 320], P(None, 'vir'), may hold values from -1 to 1
Outputs:
- residual: bfloat16 [256, 320, 320], P('occ', 'vir')
All inputs are finite; a program needn't handle non-finite values.
Results may differ from a plain program's by a relative error of at most 0.0043.
Values may be sent and summed in bfloat16 or wider, within the bound.
No kernel may reach another device: no remote copies, remote signals or barrier semaphores. Data moves between devices by JAX's collectives and lax.ppermute only.
A program may use at most 64 MiB of HBM per device.

v0:
```python
import jax
import jax.numpy as jnp
from jax import lax
from jax.sharding import PartitionSpec as P


def on_device(
    lambda_triples, amplitude_triples, spin_extent, ladder_weight, cycle_weight, lambda_doubles
):
    f32 = jnp.float32
    width = lambda_triples.shape[2]
    triples_all = lambda_triples.shape[0] * lax.axis_size("occ")
    columns = jnp.arange(width, dtype=jnp.int32)
    keep = columns[None, :] < spin_extent[:, None]
    masked = jnp.where(keep[:, None, :], lambda_triples, jnp.zeros_like(lambda_triples))
    ladder_full, doubles_full = (
        lax.all_gather(ladder_weight, "vir", axis=1, tiled=True),
        lax.all_gather(lambda_doubles, "vir", axis=1, tiled=True),
    )
    ladder_term = jnp.einsum("tae,eb->tab", masked, ladder_full, preferred_element_type=f32)
    cycle_mid = jnp.einsum(
        "tae,em->tam", amplitude_triples, cycle_weight, preferred_element_type=f32
    ).astype(jnp.bfloat16)
    cycle_term = jnp.einsum("tam,mb->tab", cycle_mid, doubles_full, preferred_element_type=f32)
    partial_density = jnp.einsum(
        "tae,tbe->ab",
        masked,
        lax.all_gather(amplitude_triples, "vir", axis=1, tiled=True),
        preferred_element_type=f32,
    )
    density = lax.psum(partial_density, "occ")
    density = (density / jnp.sqrt(f32(triples_all * width))).astype(jnp.bfloat16)
    density_term = jnp.einsum(
        "ac,tcb->tab",
        density,
        lax.all_gather(masked, "vir", axis=1, tiled=True),
        preferred_element_type=f32,
    )
    density_term = density_term / jnp.sqrt(f32(width))
    return (ladder_term + cycle_term + density_term).astype(jnp.bfloat16)


def solution(mesh):
    return jax.shard_map(
        on_device,
        mesh=mesh,
        in_specs=(
            P("occ", "vir", None),
            P("occ", "vir", None),
            P("occ"),
            P(None, "vir"),
            P(),
            P(None, "vir"),
        ),
        out_specs=P("occ", "vir", None),
        check_vma=False,
    )
```

profile of v0, /device:TPU:8, one launch (start us, length us, event | category | flops | bytes accessed | tf_op | source)
XLA Modules:
  0.0 227.4 jit_solution(11360172198900712387)
XLA Ops:
  6.5 0.0 copy-start
  6.5 0.0 copy-start.3
  6.5 0.0 copy-start.2
  6.5 0.0 all-gather.6.cloned.1.call-start
  6.5 0.7 all-gather.6.cloned.1.call-update
  7.3 0.0 all-gather.4.cloned.1.call-start
  7.3 0.7 iota_compare_fusion
  8.0 3.0 %broadcast_select_fusion = bf16[16,160,320]{2,1,0:T(8,128)(2,1)} fusion(bf16[16,160,320]{2,1,0:T(8,128)(2,1)} %param.6, pred[16,320]{1,0:T(8,128)(4,1)S(1)} %iota_compare_fusion), kind=kLoop, calls=%fused_computation.2 | loop fusion | flops 819200 | bytes 3281920 | tf_op jit(solution)/shard_map/jit(_where)/select_n | solution.py:15
  11.1 0.0 copy-start.1
  11.1 0.0 all-gather.4.cloned.1.call-update
  11.1 0.0 all-reduce.2.cloned.1.call-start
  11.2 0.0 copy-done.3
  11.2 4.6 %all-gather = bf16[2,160,40]{1,2,0:T(8,128)(2,1)S(1)} all-gather(bf16[1,160,40]{1,2,0:T(8,128)(2,1)S(1)} %bitcast.27), channel_id=1, replica_groups=mesh['occ'=16,'vir'=2] {'vir'}, dimensions={0}, use_global_device_ids=true | all-gather | bytes 38400 | tf_op jit(solution)/shard_map/all_gather | solution.py:18
  15.8 0.1 reshape.21
  15.9 0.0 copy-done.2
  15.9 6.4 %all_gather.12 = bf16[320,320]{0,1:T(8,128)(2,1)S(1)} all-gather(bf16[320,160]{0,1:T(8,128)(2,1)S(1)} %copy-done.2), channel_id=1, replica_groups=mesh['occ'=16,'vir'=2] {'vir'}, dimensions={1}, use_global_device_ids=true | all-gather | bytes 307200 | tf_op jit(solution)/shard_map/all_gather | solution.py:17
  22.3 4.9 %fusion.2 = f32[16,160,320]{2,1,0:T(8,128)} fusion(bf16[16,160,320]{2,1,0:T(8,128)(2,1)} %broadcast_select_fusion, bf16[320,320]{0,1:T(8,128)(2,1)S(1)} %all_gather.12), kind=kOutput, calls=%fused_computation.6 | convolution fusion | flops 524288000 | bytes 5120000 | tf_op jit(solution)/shard_map/tae,eb->tab/dot_general | solution.py:20
  27.2 36.7 %all-gather.6.cloned.1.call-done = bf16[16,320,320]{2,1,0:T(8,128)(2,1)} async-done(((bf16[16,160,320]{2,1,0:T(8,128)(2,1)}), bf16[16,320,320]{2,1,0:T(8,128)(2,1)}) %all-gather.6.cloned.1.call-update) | async-done | bytes 3276816 | tf_op jit(solution)/shard_map/all_gather | solution.py:28
  63.9 0.0 copy-done.1
  63.9 4.4 %convolution_bitcast_fusion = f32[160,320]{1,0:T(8,128)} fusion(bf16[16,160,320]{2,1,0:T(8,128)(2,1)S(1)} %copy-done.1, bf16[16,320,320]{2,1,0:T(8,128)(2,1)} %all-gather.6.cloned.1.call-done), kind=kOutput, calls=%fused_computation.5 | convolution fusion | flops 524288000 | bytes 5120000 | tf_op jit(solution)/shard_map/tae,tbe->ab/dot_general | solution.py:25
  68.3 0.0 all-reduce.2.cloned.1.call-update
  68.3 0.0 copy-done
  68.3 5.2 %fusion.1 = f32[16,160,320]{2,1,0:T(8,128)} fusion(bf16[320,40,1]{0,1,2:T(8,128)(2,1)S(1)} %reshape.21, bf16[16,160,320]{2,1,0:T(8,128)(2,1)} %param.7, bf16[320,40]{0,1:T(8,128)(2,1)S(1)} %copy-done), kind=kOutput, calls=%fused_computation.4 | convolution fusion | flops 131174400 | bytes 4966400 | tf_op jit(solution)/shard_map/tam,mb->tab/dot_general | solution.py:24
  73.5 46.9 %all-gather.4.cloned.1.call-done = bf16[16,320,320]{2,1,0:T(8,128)(2,1)} async-done(((bf16[16,160,320]{2,1,0:T(8,128)(2,1)}), bf16[16,320,320]{2,1,0:T(8,128)(2,1)}) %all-gather.4.cloned.1.call-update) | async-done | bytes 3276816 | tf_op jit(solution)/shard_map/all_gather | solution.py:36
  120.4 93.5 %all-reduce.2.cloned.1.call-done = f32[160,320]{1,0:T(8,128)} async-done(((f32[160,320]{1,0:T(8,128)}), f32[160,320]{1,0:T(8,128)}) %all-reduce.2.cloned.1.call-update) | async-done | bytes 204816 | tf_op jit(solution)/shard_map/psum | solution.py:31
  213.9 7.0 %fusion = bf16[16,160,320]{2,1,0:T(8,128)(2,1)} fusion(f32[16,160,320]{2,1,0:T(8,128)} %fusion.2, f32[16,160,320]{2,1,0:T(8,128)} %fusion.1, bf16[16,320,320]{2,1,0:T(8,128)(2,1)} %all-gather.4.cloned.1.call-done, f32[160,320]{1,0:T(8,128)} %all-reduce.2.cloned.1.call-done), kind=kOutput, calls=%fused_computation.1 | convolution fusion | flops 527667200 | bytes 11673600 | tf_op jit(solution)/shard_map/ac,tcb->tab/dot_general | solution.py:33
  (1 shorter events, 0.0 us)
Async XLA Ops:
  6.5 61.8 %copy-start = (bf16[320,40]{0,1:T(8,128)(2,1)S(1)}, bf16[320,40]{0,1:T(8,128)(2,1)}, u32[]{:S(2)}) copy-start(bf16[320,40]{0,1:T(8,128)(2,1)} %param.10) | copy-start | bytes 76804
  6.5 4.6 %copy-start.3 = (bf16[40,160]{1,0:T(8,128)(2,1)S(1)}, bf16[40,160]{1,0:T(8,128)(2,1)}, u32[]{:S(2)}) copy-start(bf16[40,160]{1,0:T(8,128)(2,1)} %param.11) | copy-start | bytes 38404
  6.5 9.4 %copy-start.2 = (bf16[320,160]{0,1:T(8,128)(2,1)S(1)}, bf16[320,160]{0,1:T(8,128)(2,1)}, u32[]{:S(2)}) copy-start(bf16[320,160]{0,1:T(8,128)(2,1)} %param.9) | copy-start | bytes 307204
  6.5 57.4 %all-gather.6.cloned.1.call-start = ((), (), s32[]{:S(2)}) async-start(), calls=%async_computation.1 | async-start | bytes 5898240 | tf_op jit(solution)/shard_map/all_gather | solution.py:28
  7.3 113.1 %all-gather.4.cloned.1.call-start = ((), (), s32[]{:S(2)}) async-start(), calls=%async_computation | async-start | bytes 5898240 | tf_op jit(solution)/shard_map/all_gather | solution.py:36
  11.1 52.8 %copy-start.1 = (bf16[16,160,320]{2,1,0:T(8,128)(2,1)S(1)}, bf16[16,160,320]{2,1,0:T(8,128)(2,1)}, u32[]{:S(2)}) copy-start(bf16[16,160,320]{2,1,0:T(8,128)(2,1)} %broadcast_select_fusion) | copy-start | bytes 4915204
  11.1 202.8 %all-reduce.2.cloned.1.call-start = ((), (), s32[]{:S(2)}) async-start(), calls=%async_computation.2 | async-start | bytes 491520 | tf_op jit(solution)/shard_map/psum | solution.py:31
Sparse Core Ops, SparseCore 0:
  8.9 54.9 all-gather.5
  65.4 54.8 all-gather.3
  123.8 90.0 all-reduce.1
where the time goes:
time: 228 us; the launch traced here: 227 us
  waiting for transfers between devices  178 us (78%)
  matrix products  21.4 us (9%)
  between operations  13.1 us (6%)
  blocking collectives  11 us (5%)
  other arithmetic  3.77 us (2%)
    psum x1, waiting for transfers between devices, on_device(): density = lax.psum(partial_density, 'occ')  93.5 us
    all_gather x1, waiting for transfers between devices, on_device(): lax.all_gather(masked, 'vir', axis=1, tiled=True)  46.9 us
    all_gather x1, waiting for transfers between devices, on_device(): lax.all_gather(amplitude_triples, 'vir', axis=1, tiled=True)  36.7 us
    dot_general x1, matrix products, on_device(): jnp.einsum('ac,tcb->tab', density, lax.all_gather(masked, 'vir', axis=1,...  6.97 us
    all_gather x1, blocking collectives, on_device(): lax.all_gather(ladder_weight, 'vir', axis=1, tiled=True)  6.43 us
    dot_general x1, matrix products, on_device(): jnp.einsum('tam,mb->tab', cycle_mid, doubles_full, preferred_element_type...  5.16 us
    dot_general x1, matrix products, on_device(): jnp.einsum('tae,eb->tab', masked, ladder_full, preferred_element_type=f32)  4.91 us
    all_gather x1, blocking collectives, on_device(): lax.all_gather(lambda_doubles, 'vir', axis=1, tiled=True)  4.59 us
  transfers between devices with their start and end apart: 3, of which 3 were waited for; matrix products, arithmetic and copies ran while one was open for 8% of the time, Pallas kernels for 0%

commit v1 on v0

--- a/solution.py
+++ b/solution.py
@@ -28,7 +28,11 @@
         lax.all_gather(amplitude_triples, "vir", axis=1, tiled=True),
         preferred_element_type=f32,
     )
-    density = lax.psum(partial_density, "occ")
+    density = partial_density
+    devs = lax.axis_size("occ")
+    for it in [[(p, p ^ src_i) for p in range(devs)] for src_i in (1, 2, 4, 8, 16) if src_i < devs]:
+        block_out = lax.ppermute(density, "occ", it)
+        density = density + block_out
     density = (density / jnp.sqrt(f32(triples_all * width))).astype(jnp.bfloat16)
     density_term = jnp.einsum(
         "ac,tcb->tab",

time: 228 us -> 137 us (0.60)
  waiting for transfers between devices: 178 us -> 80.6 us
  starting transfers between devices: 0.08 us -> 4.74 us
    psum x1 -> x0, waiting for transfers between devices: 93.5 us -> none  [on_device(): density = lax.psum(partial_density, 'occ')]
    all_gather x1, waiting for transfers between devices: 46.9 us -> 23.2 us  [on_device(): lax.all_gather(masked, 'vir', axis=1, tiled=True)]
    all_gather x1, waiting for transfers between devices: 36.7 us -> 52.7 us  [on_device(): lax.all_gather(amplitude_triples, 'vir', axis=1, tiled=True)]
    ppermute x0 -> x4, starting transfers between devices: none -> 4.69 us  [on_device(): block_out = lax.ppermute(density, 'occ', it)]
    ppermute x0 -> x4, waiting for transfers between devices: none -> 3.92 us  [on_device(): block_out = lax.ppermute(density, 'occ', it)]
    all_gather x1, blocking collectives: 6.43 us -> 8.74 us  [on_device(): lax.all_gather(ladder_weight, 'vir', axis=1, tiled=True)]
  transfers between devices with their start and end apart: 3 -> 6, of which waited for: 3 -> 4; matrix products, arithmetic and copies ran while one was open for 8% -> 12% of each run, Pallas kernels for 0% -> 0%
where the time goes in v1:
time: 137 us; the launch traced here: 136 us
  waiting for transfers between devices  80.6 us (59%)
  matrix products  19.6 us (14%)
  between operations  13.5 us (10%)
  blocking collectives  13.2 us (10%)
  starting transfers between devices  4.74 us (3%)
  other arithmetic  3.85 us (3%)
    all_gather x1, waiting for transfers between devices, on_device(): lax.all_gather(amplitude_triples, 'vir', axis=1, tiled=True)  52.7 us
    all_gather x1, waiting for transfers between devices, on_device(): lax.all_gather(masked, 'vir', axis=1, tiled=True)  23.2 us
    all_gather x1, blocking collectives, on_device(): lax.all_gather(ladder_weight, 'vir', axis=1, tiled=True)  8.74 us
    dot_general x1, matrix products, on_device(): jnp.einsum('ac,tcb->tab', density, lax.all_gather(masked, 'vir', axis=1,...  6.91 us
    dot_general x1, matrix products, on_device(): jnp.einsum('tam,mb->tab', cycle_mid, doubles_full, preferred_element_type...  5.14 us
    ppermute x4, starting transfers between devices, on_device(): block_out = lax.ppermute(density, 'occ', it)  4.69 us
    all_gather x1, blocking collectives, on_device(): lax.all_gather(lambda_doubles, 'vir', axis=1, tiled=True)  4.45 us
    dot_general x1, matrix products, on_device(): jnp.einsum('tae,tbe->ab', masked, lax.all_gather(amplitude_triples, 'vir'...  4.32 us
  transfers between devices with their start and end apart: 6, of which 4 were waited for; matrix products, arithmetic and copies ran while one was open for 12% of the time, Pallas kernels for 0%

profile of v1, /device:TPU:8, one launch (start us, length us, event | category | flops | bytes accessed | tf_op | source)
XLA Modules:
  0.0 135.6 jit_solution(12270968385151010080)
XLA Ops:
  6.5 0.0 copy-start
  6.5 0.0 all-gather.6.cloned.1.call-start
  6.5 0.7 all-gather.6.cloned.1.call-update
  7.3 0.0 all-gather.4.cloned.1.call-start
  7.3 0.7 iota_compare_fusion
  8.0 3.0 %broadcast_select_fusion = bf16[16,160,320]{2,1,0:T(8,128)(2,1)} fusion(bf16[16,160,320]{2,1,0:T(8,128)(2,1)} %param.6, pred[16,320]{1,0:T(8,128)(4,1)S(1)} %iota_compare_fusion), kind=kLoop, calls=%fused_computation.2 | loop fusion | flops 819200 | bytes 3281920 | tf_op jit(solution)/shard_map/jit(_where)/select_n | solution.py:15
  11.1 0.0 all-gather.4.cloned.1.call-update
  11.1 0.0 copy-start.3
  11.1 0.0 copy-start.2
  11.1 0.0 copy-start.1
  11.1 52.7 %all-gather.6.cloned.1.call-done = bf16[16,320,320]{2,1,0:T(8,128)(2,1)} async-done(((bf16[16,160,320]{2,1,0:T(8,128)(2,1)}), bf16[16,320,320]{2,1,0:T(8,128)(2,1)}) %all-gather.6.cloned.1.call-update) | async-done | bytes 3276816 | tf_op jit(solution)/shard_map/all_gather | solution.py:28
  63.9 4.3 %convolution_bitcast_fusion = f32[160,320]{1,0:T(8,128)S(1)} fusion(bf16[16,160,320]{2,1,0:T(8,128)(2,1)} %broadcast_select_fusion, bf16[16,320,320]{2,1,0:T(8,128)(2,1)} %all-gather.6.cloned.1.call-done), kind=kOutput, calls=%fused_computation.5 | convolution fusion | flops 524288000 | bytes 5120000 | tf_op jit(solution)/shard_map/tae,tbe->ab/dot_general | solution.py:25
  68.2 0.1 collective-permute-start
  68.3 1.5 %collective-permute-done = f32[160,320]{1,0:T(8,128)S(1)} collective-permute-done((f32[160,320]{1,0:T(8,128)S(1)}, f32[160,320]{1,0:T(8,128)S(1)}, u32[]{:S(2)}, u32[]{:S(2)}) %collective-permute-start) | collective-permute-done | bytes 204832 | tf_op jit(solution)/shard_map/ppermute | solution.py:34
  69.8 1.5 %collective-permute-start.1 = (f32[160,320]{1,0:T(8,128)S(1)}, f32[160,320]{1,0:T(8,128)S(1)}, u32[]{:S(2)}, u32[]{:S(2)}) collective-permute-start(f32[160,320]{1,0:T(8,128)S(1)} %add.19), channel_id=1, source_target_pairs={{0,4},{2,6},{4,0},{6,2},{8,12},{10,14},{12,8},{14,10},{16,20},{18,... | collective-permute-start | bytes 614408 | tf_op jit(solution)/shard_map/ppermute | solution.py:34
  71.4 0.0 copy-done.3
  71.4 4.4 %all-gather = bf16[2,160,40]{1,2,0:T(8,128)(2,1)S(1)} all-gather(bf16[1,160,40]{1,2,0:T(8,128)(2,1)S(1)} %bitcast.27), channel_id=1, replica_groups=mesh['occ'=16,'vir'=2] {'vir'}, dimensions={0}, use_global_device_ids=true | all-gather | bytes 38400 | tf_op jit(solution)/shard_map/all_gather | solution.py:18
  75.8 0.1 reshape.21
  75.9 0.0 copy-done.2
  75.9 8.7 %all_gather.12 = bf16[320,320]{0,1:T(8,128)(2,1)S(1)} all-gather(bf16[320,160]{0,1:T(8,128)(2,1)S(1)} %copy-done.2), channel_id=1, replica_groups=mesh['occ'=16,'vir'=2] {'vir'}, dimensions={1}, use_global_device_ids=true | all-gather | bytes 307200 | tf_op jit(solution)/shard_map/all_gather | solution.py:17
  84.7 0.0 collective-permute-done.1
  84.7 0.6 collective-permute-start.2
  85.3 0.0 copy-done.1
  85.3 3.2 %fusion.2 = f32[16,160,320]{2,1,0:T(8,128)} fusion(bf16[16,160,320]{2,1,0:T(8,128)(2,1)S(1)} %copy-done.1, bf16[320,320]{0,1:T(8,128)(2,1)S(1)} %all_gather.12), kind=kOutput, calls=%fused_computation.6 | convolution fusion | flops 524288000 | bytes 5120000 | tf_op jit(solution)/shard_map/tae,eb->tab/dot_general | solution.py:20
  88.6 2.4 %collective-permute-done.2 = f32[160,320]{1,0:T(8,128)S(1)} collective-permute-done((f32[160,320]{1,0:T(8,128)S(1)}, f32[160,320]{1,0:T(8,128)S(1)}, u32[]{:S(2)}, u32[]{:S(2)}) %collective-permute-start.2) | collective-permute-done | bytes 204832 | tf_op jit(solution)/shard_map/ppermute | solution.py:34
  91.0 2.5 %collective-permute-start.3 = (f32[160,320]{1,0:T(8,128)S(1)}, f32[160,320]{1,0:T(8,128)S(1)}, u32[]{:S(2)}, u32[]{:S(2)}) collective-permute-start(f32[160,320]{1,0:T(8,128)S(1)} %add.21), channel_id=1, source_target_pairs={{0,16},{2,18},{4,20},{6,22},{8,24},{10,26},{12,28},{14,30},{16,0},... | collective-permute-start | bytes 614408 | tf_op jit(solution)/shard_map/ppermute | solution.py:34
  93.5 0.0 copy-done
  93.5 5.1 %fusion.1 = f32[16,160,320]{2,1,0:T(8,128)} fusion(bf16[320,40,1]{0,1,2:T(8,128)(2,1)S(1)} %reshape.21, bf16[16,160,320]{2,1,0:T(8,128)(2,1)} %param.7, bf16[320,40]{0,1:T(8,128)(2,1)S(1)} %copy-done), kind=kOutput, calls=%fused_computation.4 | convolution fusion | flops 131174400 | bytes 4966400 | tf_op jit(solution)/shard_map/tam,mb->tab/dot_general | solution.py:24
  98.6 23.2 %all-gather.4.cloned.1.call-done = bf16[16,320,320]{2,1,0:T(8,128)(2,1)} async-done(((bf16[16,160,320]{2,1,0:T(8,128)(2,1)}), bf16[16,320,320]{2,1,0:T(8,128)(2,1)}) %all-gather.4.cloned.1.call-update) | async-done | bytes 3276816 | tf_op jit(solution)/shard_map/all_gather | solution.py:40
  121.9 0.0 collective-permute-done.3
  121.9 6.9 %fusion = bf16[16,160,320]{2,1,0:T(8,128)(2,1)} fusion(f32[16,160,320]{2,1,0:T(8,128)} %fusion.2, f32[16,160,320]{2,1,0:T(8,128)} %fusion.1, bf16[16,320,320]{2,1,0:T(8,128)(2,1)} %all-gather.4.cloned.1.call-done, f32[160,320]{1,0:T(8,128)S(1)} %add.21, f32[160,320]{1,0:T(8,128)S(1)} %collective-permute-done.3), kind=kOutput, calls=%fused_computation.1 | convolution fusion | flops 527718400 | bytes 11878400 | tf_op jit(solution)/shard_map/ac,tcb->tab/dot_general | solution.py:37
  (4 shorter events, 0.1 us)
Async XLA Ops:
  6.5 87.0 %copy-start = (bf16[320,40]{0,1:T(8,128)(2,1)S(1)}, bf16[320,40]{0,1:T(8,128)(2,1)}, u32[]{:S(2)}) copy-start(bf16[320,40]{0,1:T(8,128)(2,1)} %param.10) | copy-start | bytes 76804
  6.5 57.4 %all-gather.6.cloned.1.call-start = ((), (), s32[]{:S(2)}) async-start(), calls=%async_computation.1 | async-start | bytes 5898240 | tf_op jit(solution)/shard_map/all_gather | solution.py:28
  7.3 114.6 %all-gather.4.cloned.1.call-start = ((), (), s32[]{:S(2)}) async-start(), calls=%async_computation | async-start | bytes 5898240 | tf_op jit(solution)/shard_map/all_gather | solution.py:40
  11.1 60.3 %copy-start.3 = (bf16[40,160]{1,0:T(8,128)(2,1)S(1)}, bf16[40,160]{1,0:T(8,128)(2,1)}, u32[]{:S(2)}) copy-start(bf16[40,160]{1,0:T(8,128)(2,1)} %param.11) | copy-start | bytes 38404
  11.1 64.8 %copy-start.2 = (bf16[320,160]{0,1:T(8,128)(2,1)S(1)}, bf16[320,160]{0,1:T(8,128)(2,1)}, u32[]{:S(2)}) copy-start(bf16[320,160]{0,1:T(8,128)(2,1)} %param.9) | copy-start | bytes 307204
  11.1 74.2 %copy-start.1 = (bf16[16,160,320]{2,1,0:T(8,128)(2,1)S(1)}, bf16[16,160,320]{2,1,0:T(8,128)(2,1)}, u32[]{:S(2)}) copy-start(bf16[16,160,320]{2,1,0:T(8,128)(2,1)} %broadcast_select_fusion) | copy-start | bytes 4915204
  68.2 1.6 %collective-permute-start = (f32[160,320]{1,0:T(8,128)S(1)}, f32[160,320]{1,0:T(8,128)S(1)}, u32[]{:S(2)}, u32[]{:S(2)}) collective-permute-start(f32[160,320]{1,0:T(8,128)S(1)} %convolution_bitcast_fusion), channel_id=1, source_target_pairs={{0,2},{2,0},{4,6},{6,4},{8,10},{10,8},{12,14},{14,12},{16,18},{18,... | collective-permute-start | bytes 614408 | tf_op jit(solution)/shard_map/ppermute | solution.py:34
  69.8 14.9 %collective-permute-start.1 = (f32[160,320]{1,0:T(8,128)S(1)}, f32[160,320]{1,0:T(8,128)S(1)}, u32[]{:S(2)}, u32[]{:S(2)}) collective-permute-start(f32[160,320]{1,0:T(8,128)S(1)} %add.19), channel_id=1, source_target_pairs={{0,4},{2,6},{4,0},{6,2},{8,12},{10,14},{12,8},{14,10},{16,20},{18,... | collective-permute-start | bytes 614408 | tf_op jit(solution)/shard_map/ppermute | solution.py:34
  84.7 6.3 %collective-permute-start.2 = (f32[160,320]{1,0:T(8,128)S(1)}, f32[160,320]{1,0:T(8,128)S(1)}, u32[]{:S(2)}, u32[]{:S(2)}) collective-permute-start(f32[160,320]{1,0:T(8,128)S(1)} %add.20), channel_id=1, source_target_pairs={{0,8},{2,10},{4,12},{6,14},{8,0},{10,2},{12,4},{14,6},{16,24},{18,... | collective-permute-start | bytes 614408 | tf_op jit(solution)/shard_map/ppermute | solution.py:34
  91.0 30.9 %collective-permute-start.3 = (f32[160,320]{1,0:T(8,128)S(1)}, f32[160,320]{1,0:T(8,128)S(1)}, u32[]{:S(2)}, u32[]{:S(2)}) collective-permute-start(f32[160,320]{1,0:T(8,128)S(1)} %add.21), channel_id=1, source_target_pairs={{0,16},{2,18},{4,20},{6,22},{8,24},{10,26},{12,28},{14,30},{16,0},... | collective-permute-start | bytes 614408 | tf_op jit(solution)/shard_map/ppermute | solution.py:34
Sparse Core Ops, SparseCore 0:
  8.9 54.9 all-gather.5
  65.4 56.4 all-gather.3
